TPU v7x, 256 devices: a whole 4x4x8 slice. The times are simulated.
256 devices in a mesh: ctx: 8 (over x, y_hi), chan: 32 (over z, y_lo, core).
Axes of the slice: x: 4, y: 4 (y_hi: 2, y_lo: 2; y = y_hi * 2 + y_lo), z: 8, core: 2. Of those that a mesh axis runs over, the one named last changes fastest.
Arguments:
- inputs: bfloat16 [4096, 4096], P('ctx', 'chan'), may hold values from -6 to 6
- w_in: bfloat16 [4096, 3, 4096], P(None, None, 'chan'), may hold values from -0.09375 to 0.09375
- conv_taps: bfloat16 [3, 3, 4096], P(None, None, 'chan'), may hold values from -3.59375 to 3.59375
- skip_gain: float32 [4096], P('chan'), may hold values from 0.5 to 1.5
- filter_taps: bfloat16 [4096, 4096], P('ctx', 'chan'), may hold values from -0.09375 to 0.09375
- w_out: bfloat16 [4096, 4096], P('chan'), may hold values from -0.1875 to 0.1875
Outputs:
- result: bfloat16 [4096, 4096], P('ctx', 'chan')
All inputs are finite; a program needn't handle non-finite values.
Results may differ from a plain program's by a relative error of at most 0.024.
Values may be sent and summed in bfloat16 or wider, within the bound.
A program may use at most 64 MiB of HBM per device.

v0:
```python
import math
import jax
import jax.numpy as jnp
from jax import lax
from jax.sharding import PartitionSpec as P

KERNEL = 3


def dft_table(double_len):
    step = 32
    hi_ids = jnp.arange(double_len // step, dtype=jnp.int32)[:, None]
    lo_ids = jnp.arange(step, dtype=jnp.int32)[:, None]
    cols = jnp.arange(double_len, dtype=jnp.int32)[None, :]
    scale = 2.0 * math.pi / double_len
    hi_angle = scale * (hi_ids * step * cols % double_len).astype(jnp.float32)
    lo_angle = scale * (lo_ids * cols % double_len).astype(jnp.float32)
    hc, hs = (jnp.cos(hi_angle)[:, None], jnp.sin(hi_angle)[:, None])
    lc, ls = (jnp.cos(lo_angle)[None], jnp.sin(lo_angle)[None])
    cos = (hc * lc - hs * ls).reshape(double_len, double_len)
    sin = (hs * lc + hc * ls).reshape(double_len, double_len)
    return jnp.concatenate([cos, -sin], 0).astype(jnp.bfloat16)


def body(inputs, w_in, conv_taps, skip_gain, filter_taps, w_out):
    span_len, width_dev = inputs.shape
    double_len = 2 * span_len
    groups = lax.axis_size("ctx")
    position = lax.axis_index("ctx")
    own = width_dev // groups
    with jax.named_scope("out_weight_columns"):
        w_cols = lax.all_to_all(w_out, "chan", 1, 0, tiled=True)
    with jax.named_scope("filter_to_owner"):
        taps_t = filter_taps.T.reshape(groups, own, span_len)
        taps_t = lax.all_to_all(taps_t, "ctx", 0, 0, tiled=True)
    with jax.named_scope("input_projection"):
        inputs_t = lax.all_gather(inputs.T, "chan", axis=0, tiled=True)
        w_flat = w_in.reshape(w_in.shape[0], 3 * width_dev)
        proj_t = lax.dot_general(
            w_flat, inputs_t, (((0,), (0,)), ((), ())), preferred_element_type=jnp.float32
        ).astype(jnp.bfloat16)
    with jax.named_scope("projection_to_owner"):
        proj_t = proj_t.reshape(3, groups, own, span_len)
        proj_t = lax.all_to_all(proj_t, "ctx", 1, 1, tiled=True)
    with jax.named_scope("short_conv"):
        start = position * own
        taps = lax.dynamic_slice_in_dim(conv_taps, start, own, axis=2)
        rim = jnp.pad(
            proj_t[:, :-1, :, span_len - (KERNEL - 1) :], ((0, 0), (1, 0), (0, 0), (0, 0))
        )
        padded = jnp.concatenate([rim, proj_t], 3)
        filtered = jnp.zeros(proj_t.shape, jnp.float32)
        for lag in range(KERNEL):
            start_row = KERNEL - 1 - lag
            filtered = filtered + taps[lag].astype(jnp.float32)[:, None, :, None] * padded[
                ..., start_row : start_row + span_len
            ].astype(jnp.float32)
        streams = filtered.astype(jnp.bfloat16)
        gate_out = streams[0]
        gated_in = (streams[1].astype(jnp.float32) * streams[2].astype(jnp.float32)).astype(
            jnp.bfloat16
        )
    with jax.named_scope("spectra"):
        table = dft_table(double_len)
        forward_in = table[:, :span_len]
        spectra_in = jnp.einsum(
            "jdb,fb->jdf", gated_in, forward_in, preferred_element_type=jnp.float32
        ).astype(jnp.bfloat16)
        previous = jnp.pad(taps_t[:-1, :, 1:], ((1, 0), (0, 0), (0, 0)))
        padded_taps = jnp.concatenate(
            [taps_t, jnp.zeros((groups, own, 1), jnp.bfloat16), previous], 2
        )
        spectra_taps = jnp.einsum(
            "kdm,fm->kdf", padded_taps, table, preferred_element_type=jnp.float32
        ).astype(jnp.bfloat16)
    with jax.named_scope("mixture"):
        real_g = spectra_taps[:, :, :double_len].astype(jnp.float32)
        imag_g = spectra_taps[:, :, double_len:].astype(jnp.float32)
        real_u = spectra_in[:, :, :double_len].astype(jnp.float32)
        imag_u = spectra_in[:, :, double_len:].astype(jnp.float32)
        mixed = []
        for target in range(groups):
            acc_r = jnp.zeros((own, double_len), jnp.float32)
            acc_i = jnp.zeros((own, double_len), jnp.float32)
            for source in range(target + 1):
                lag = target - source
                acc_r = acc_r + (real_g[lag] * real_u[source] - imag_g[lag] * imag_u[source])
                acc_i = acc_i + (real_g[lag] * imag_u[source] + imag_g[lag] * real_u[source])
            mixed.append(jnp.concatenate([acc_r, acc_i], 1))
        mixture = jnp.stack(mixed, 0).astype(jnp.bfloat16)
    with jax.named_scope("inverse_and_gate"):
        long_out = jnp.einsum(
            "idf,fa->ida", mixture, forward_in, preferred_element_type=jnp.float32
        ) * (1.0 / double_len)
        gain = lax.dynamic_slice_in_dim(skip_gain, start, own)
        long_out = long_out + gain[None, :, None] * gated_in.astype(jnp.float32)
        gated_out = (gate_out.astype(jnp.float32) * long_out).astype(jnp.bfloat16)
    with jax.named_scope("gated_back_to_rows"):
        gated_out = lax.all_to_all(gated_out, "ctx", 0, 0, tiled=True)
        gated_out = gated_out.reshape(width_dev, span_len)
    with jax.named_scope("output_projection"):
        gathered = lax.all_gather(gated_out, "chan", axis=0, tiled=True)
        result = lax.dot_general(
            gathered, w_cols, (((0,), (0,)), ((), ())), preferred_element_type=jnp.float32
        ).astype(jnp.bfloat16)
    return result


def solution(mesh):
    return jax.shard_map(
        body,
        mesh=mesh,
        in_specs=(
            P("ctx", "chan"),
            P(None, None, "chan"),
            P(None, None, "chan"),
            P("chan"),
            P("ctx", "chan"),
            P("chan", None),
        ),
        out_specs=P("ctx", "chan"),
        check_vma=False,
    )
```

profile of v0, /device:TPU:1, one launch (start us, length us, event | category | flops | bytes accessed | tf_op | source)
XLA Modules:
  0.0 208.1 jit_solution(4928286048202900547)
XLA Ops:
  6.5 0.0 all-gather.3.cloned.1.call-start
  6.5 0.7 all-gather.3.cloned.1.call-update
  7.3 1.9 copy.19
  9.1 7.5 %all-to-all-start.1 = ((bf16[8,16,512]{2,1,0:T(8,128)(2,1)}), bf16[8,16,512]{2,1,0:T(8,128)(2,1)S(1)}, u32[]{:S(2)}, u32[]{:S(2)}) async-start(bf16[8,16,512]{2,1,0:T(8,128)(2,1)} %bitcast.8), calls=%async_computation.1 | async-start | bytes 262144 | tf_op jit(solution)/shard_map/filter_to_owner/all_to_all | solution.py:35
  16.6 0.5 fusion.45
  17.2 0.6 fusion.48
  17.8 3.5 %negate_convert_fusion = (bf16[32,32,1024]{2,1,0:T(8,128)(2,1)}, bf16[32,32,1024]{2,1,0:T(8,128)(2,1)}) fusion(f32[32,1024]{1,0:T(8,128)S(1)} %get-tuple-element.22, f32[32,1024]{1,0:T(8,128)S(1)} %get-tuple-element.21, f32[32,1024]{1,0:T(8,128)S(1)} %get-tuple-element.23, f32[32,1024]{1,0:T(8,128)S(1)} %get-tuple-element.20), kind=kLoop, calls=%fused_computation.5 | loop fusion | flops 9437184 | bytes 4718592 | tf_op jit(solution)/shard_map/convert.44
  21.3 2.9 %copy.14 = bf16[4096,3,128]{0,2,1:T(8,128)(2,1)} copy(bf16[4096,3,128]{2,0,1:T(8,128)(2,1)S(1)} %copy-done) | data formatting | bytes 6291456 | tf_op args[1]
  24.2 0.1 dynamic_slice.7
  24.3 0.0 copy-done.5
  24.3 0.1 fusion.68
  24.3 0.0 all-to-all-done.1
  24.4 0.1 slice.145
  24.5 61.2 %all-gather.3.cloned.1.call-done = bf16[4096,512]{0,1:T(8,128)(2,1)} async-done(((bf16[128,512]{0,1:T(8,128)(2,1)}), bf16[4096,512]{0,1:T(8,128)(2,1)}) %all-gather.3.cloned.1.call-update) | async-done | bytes 4194320 | tf_op jit(solution)/shard_map/input_projection/all_gather | solution.py:37
  85.6 5.1 %convolution_convert_fusion.1 = bf16[384,512]{1,0:T(8,128)(2,1)S(1)} fusion(bf16[4096,384]{0,1:T(8,128)(2,1)} %bitcast.117, bf16[4096,512]{0,1:T(8,128)(2,1)} %all-gather.3.cloned.1.call-done), kind=kOutput, calls=%fused_computation.11 | convolution fusion | flops 1610809344 | bytes 7733248 | tf_op jit(solution)/shard_map/input_projection/dot_general | solution.py:39
  90.7 0.8 copy.15
  91.5 6.4 %all-to-all-start = ((bf16[3,8,16,512]{3,2,0,1:T(8,128)(2,1)}), bf16[3,8,16,512]{3,2,0,1:T(8,128)(2,1)S(1)}, u32[]{:S(2)}, u32[]{:S(2)}) async-start(bf16[3,8,16,512]{3,2,0,1:T(8,128)(2,1)} %copy.15), calls=%async_computation | async-start | bytes 786432 | tf_op jit(solution)/shard_map/projection_to_owner/all_to_all | solution.py:44
  97.9 0.0 all-gather.5.cloned.1.call-start
  97.9 3.2 %fusion.3 = bf16[8,16,2048]{2,1,0:T(8,128)(2,1)S(1)} fusion(bf16[1024,1024]{1,0:T(8,128)(2,1)S(1)} %bitcast.118, bf16[1024,1024]{1,0:T(8,128)(2,1)} %bitcast.121, bf16[7,16,511]{2,1,0:T(8,128)(2,1)S(1)} %slice.145, bf16[8,16,512]{2,1,0:T(8,128)(2,1)} %copy-done.4, bf16[1024]{0:T(1024)(128)(2,1)S(1)} %pad.29.clone), kind=kOutput, calls=%fused_computation.7 | convolution fusion | flops 546570240 | bytes 4966176 | tf_op jit(solution)/shard_map/spectra/kdm,fm->kdf/dot_general | solution.py:73
  101.1 0.1 slice_convert_fusion.3
  101.2 6.1 %all-to-all-done = bf16[3,8,16,512]{3,2,0,1:T(8,128)(2,1)S(1)} async-done(((bf16[3,8,16,512]{3,2,0,1:T(8,128)(2,1)}), bf16[3,8,16,512]{3,2,0,1:T(8,128)(2,1)S(1)}, u32[]{:S(2)}, u32[]{:S(2)}) %all-to-all-start) | async-done | bytes 393248 | tf_op jit(solution)/shard_map/projection_to_owner/all_to_all | solution.py:44
  107.3 0.1 slice.141
  107.4 0.2 fusion.13
  107.7 0.4 add_convert_fusion
  108.0 2.0 convolution_convert_fusion
  110.1 0.1 slice_convert_fusion.2
  110.2 0.2 fusion.63
  110.4 0.2 fusion.64
  110.5 0.1 fusion.61
  110.7 0.1 fusion.62
  110.8 0.1 fusion.59
  110.9 0.1 fusion.60
  111.1 0.1 fusion.57
  111.1 0.1 fusion.58
  111.2 0.1 fusion.55
  111.3 0.1 fusion.56
  111.4 0.1 fusion.54
  111.5 0.1 fusion.53
  111.5 0.0 copy-start.3
  111.7 1.0 copy-done.2
  112.6 0.5 fusion.10
  113.1 9.8 %all_to_all.34 = bf16[8,16,512]{2,1,0:T(8,128)(2,1)} all-to-all(bf16[8,16,512]{2,1,0:T(8,128)(2,1)S(1)} %fusion.10), channel_id=1, replica_groups=mesh['ctx'=8,'chan'=32] {'ctx'}, dimensions={0} | all-to-all | bytes 262144 | tf_op jit(solution)/shard_map/gated_back_to_rows/all_to_all | solution.py:99
  122.9 0.0 all-gather.5.cloned.1.call-update
  123.0 0.7 copy.20
  123.7 44.2 %all_to_all.35 = bf16[128,32,128]{0,2,1:T(8,128)(2,1)S(1)} all-to-all(bf16[128,32,128]{0,2,1:T(8,128)(2,1)S(1)} %bitcast.116), channel_id=1, replica_groups=mesh['ctx'=8,'chan'=32] {'chan'}, dimensions={1} | all-to-all | bytes 2097152 | tf_op jit(solution)/shard_map/out_weight_columns/all_to_all | solution.py:32
  167.9 0.7 copy.21
  168.6 28.6 %all-gather.5.cloned.1.call-done = bf16[4096,512]{1,0:T(8,128)(2,1)} async-done(((bf16[128,512]{1,0:T(8,128)(2,1)}), bf16[4096,512]{1,0:T(8,128)(2,1)}) %all-gather.5.cloned.1.call-update) | async-done | bytes 4194320 | tf_op jit(solution)/shard_map/output_projection/all_gather | solution.py:102
  197.1 4.1 %convolution_convert_fusion.2 = bf16[512,128]{1,0:T(8,128)(2,1)} fusion(bf16[4096,512]{1,0:T(8,128)(2,1)} %all-gather.5.cloned.1.call-done, bf16[4096,128]{1,0:T(8,128)(2,1)S(1)} %bitcast.124), kind=kOutput, calls=%fused_computation.15 | convolution fusion | flops 536936448 | bytes 5373952 | tf_op jit(solution)/shard_map/output_projection/dot_general | solution.py:103
  (23 shorter events, 0.1 us)
Async XLA Ops:
  6.5 14.8 %copy-start = (bf16[4096,3,128]{2,0,1:T(8,128)(2,1)S(1)}, bf16[4096,3,128]{2,0,1:T(8,128)(2,1)}, u32[]{:S(2)}) copy-start(bf16[4096,3,128]{2,0,1:T(8,128)(2,1)} %param.7) | copy-start | bytes 9437188
  6.5 79.1 %all-gather.3.cloned.1.call-start = ((), (), s32[]{:S(2)}) async-start(), calls=%async_computation.4 | async-start | bytes 4325376 | tf_op jit(solution)/shard_map/input_projection/all_gather | solution.py:37
  9.1 15.2 %all-to-all-start.1 = ((bf16[8,16,512]{2,1,0:T(8,128)(2,1)}), bf16[8,16,512]{2,1,0:T(8,128)(2,1)S(1)}, u32[]{:S(2)}, u32[]{:S(2)}) async-start(bf16[8,16,512]{2,1,0:T(8,128)(2,1)} %bitcast.8), calls=%async_computation.1 | async-start | bytes 262144 | tf_op jit(solution)/shard_map/filter_to_owner/all_to_all | solution.py:35
  21.3 2.9 %copy-start.6 = (f32[128]{0:T(128)S(1)}, f32[128]{0:T(128)}, u32[]{:S(2)}) copy-start(f32[128]{0:T(128)} %param.9) | copy-start | bytes 1540
  21.3 3.0 %copy-start.5 = (bf16[3,3,128]{2,1,0:T(4,128)(2,1)S(1)}, bf16[3,3,128]{2,1,0:T(4,128)(2,1)}, u32[]{:S(2)}) copy-start(bf16[3,3,128]{2,1,0:T(4,128)(2,1)} %param.8) | copy-start | bytes 6916
  24.4 66.4 %copy-start.4 = (bf16[8,16,512]{2,1,0:T(8,128)(2,1)}, bf16[8,16,512]{2,1,0:T(8,128)(2,1)S(1)}, u32[]{:S(2)}) copy-start(bf16[8,16,512]{2,1,0:T(8,128)(2,1)S(1)} %all-to-all-done.1) | copy-start | bytes 393220
  85.6 12.3 %copy-start.1 = (bf16[32,32,1024]{2,1,0:T(8,128)(2,1)S(1)}, bf16[32,32,1024]{2,1,0:T(8,128)(2,1)}, u32[]{:S(2)}) copy-start(bf16[32,32,1024]{2,1,0:T(8,128)(2,1)} %get-tuple-element.15) | copy-start | bytes 6291460
  91.5 15.8 %all-to-all-start = ((bf16[3,8,16,512]{3,2,0,1:T(8,128)(2,1)}), bf16[3,8,16,512]{3,2,0,1:T(8,128)(2,1)S(1)}, u32[]{:S(2)}, u32[]{:S(2)}) async-start(bf16[3,8,16,512]{3,2,0,1:T(8,128)(2,1)} %copy.15), calls=%async_computation | async-start | bytes 786432 | tf_op jit(solution)/shard_map/projection_to_owner/all_to_all | solution.py:44
  97.9 99.3 %all-gather.5.cloned.1.call-start = ((), (), s32[]{:S(2)}) async-start(), calls=%async_computation.5 | async-start | bytes 4325376 | tf_op jit(solution)/shard_map/output_projection/all_gather | solution.py:102
  111.1 1.6 copy-start.2
  111.5 11.4 %copy-start.3 = (bf16[128,4096]{1,0:T(8,128)(2,1)S(1)}, bf16[128,4096]{1,0:T(8,128)(2,1)}, u32[]{:S(2)}) copy-start(bf16[128,4096]{1,0:T(8,128)(2,1)} %param.11) | copy-start | bytes 3145732
Sparse Core Ops, SparseCore 0:
  9.1 76.4 all-gather.2
  123.1 74.0 all-gather.4
where the time goes:
time: 209 us; the launch traced here: 208 us
  waiting for transfers between devices  96.6 us (46%)
  blocking collectives  54.1 us (26%)
  matrix products  14.9 us (7%)
  starting transfers between devices  13.9 us (7%)
  between operations  13.7 us (7%)
  local copies, waits for them, and re-layouts  8.15 us (4%)
  other arithmetic  6.84 us (3%)
    all_gather x1, waiting for transfers between devices, body(): inputs_t = lax.all_gather(inputs.T, 'chan', axis=0, tiled=True)  61.2 us
    all_to_all x1, blocking collectives, body(): w_cols = lax.all_to_all(w_out, 'chan', 1, 0, tiled=True)  44.2 us
    all_gather x1, waiting for transfers between devices, body(): gathered = lax.all_gather(gated_out, 'chan', axis=0, tiled=True)  28.6 us
    all_to_all x1, blocking collectives, body(): gated_out = lax.all_to_all(gated_out, 'ctx', 0, 0, tiled=True)  9.83 us
    all_to_all x1, starting transfers between devices, body(): taps_t = lax.all_to_all(taps_t, 'ctx', 0, 0, tiled=True)  7.48 us
    all_to_all x1, starting transfers between devices, body(): proj_t = lax.all_to_all(proj_t, 'ctx', 1, 1, tiled=True)  6.35 us
    all_to_all x1, waiting for transfers between devices, body(): proj_t = lax.all_to_all(proj_t, 'ctx', 1, 1, tiled=True)  6.07 us
    dot_general x1, matrix products, body(): lax.dot_general(w_flat, inputs_t, (((0,), (0,)), ((), ())), preferred_ele...  5.1 us
  transfers between devices with their start and end apart: 4, of which 3 were waited for; matrix products, arithmetic and copies ran while one was open for 7% of the time, Pallas kernels for 0%

commit v1 on v0

--- a/solution.py
+++ b/solution.py
@@ -99,7 +99,9 @@
         gated_out = lax.all_to_all(gated_out, "ctx", 0, 0, tiled=True)
         gated_out = gated_out.reshape(width_dev, span_len)
     with jax.named_scope("output_projection"):
-        gathered = lax.all_gather(gated_out, "chan", axis=0, tiled=True)
+        gathered = jnp.concatenate(
+            lax.all_to_all(jnp.stack([gated_out] * lax.axis_size("chan")), "chan", 0, 0), axis=0
+        )
         result = lax.dot_general(
             gathered, w_cols, (((0,), (0,)), ((), ())), preferred_element_type=jnp.float32
         ).astype(jnp.bfloat16)

time: 209 us -> 269 us (1.29)
  blocking collectives: 54.1 us -> 99.6 us
  starting transfers between devices: 13.9 us -> 24.1 us
  waiting for transfers between devices: 96.6 us -> 101 us
    all_to_all x2 -> x1, blocking collectives: 54.1 us -> 99.6 us  [body(): lax.all_to_all(jnp.stack([gated_out] * lax.axis_size('chan')), 'chan', 0, 0)]
    all_to_all x0 -> x2, waiting for transfers between devices: none -> 32.7 us  [the longest x1 28 us: body(): w_cols = lax.all_to_all(w_out, 'chan', 1, 0, tiled=True)]
    all_gather x1 -> x0, waiting for transfers between devices: 28.6 us -> none  [body(): gathered = lax.all_gather(gated_out, 'chan', axis=0, tiled=True)]
    all_to_all x0 -> x2, starting transfers between devices: none -> 10.3 us  [the longest x1 6.9 us: body(): w_cols = lax.all_to_all(w_out, 'chan', 1, 0, tiled=True)]
  transfers between devices with their start and end apart: 4 -> 5, of which waited for: 3 -> 4; matrix products, arithmetic and copies ran while one was open for 7% -> 6% of each run, Pallas kernels for 0% -> 0%
where the time goes in v1:
time: 269 us; the launch traced here: 268 us
  waiting for transfers between devices  101 us (38%)
  blocking collectives  99.6 us (37%)
  starting transfers between devices  24.1 us (9%)
  between operations  13.7 us (5%)
  matrix products  13.4 us (5%)
  local copies, waits for them, and re-layouts  9.89 us (4%)
  other arithmetic  6.84 us (3%)
    all_to_all x1, blocking collectives, body(): lax.all_to_all(jnp.stack([gated_out] * lax.axis_size('chan')), 'chan', 0, 0)  99.6 us
    all_gather x1, waiting for transfers between devices, body(): inputs_t = lax.all_gather(inputs.T, 'chan', axis=0, tiled=True)  61.2 us
    all_to_all x1, waiting for transfers between devices, body(): w_cols = lax.all_to_all(w_out, 'chan', 1, 0, tiled=True)  28 us
    all_to_all x1, starting transfers between devices, body(): taps_t = lax.all_to_all(taps_t, 'ctx', 0, 0, tiled=True)  7.48 us
    all_to_all x1, starting transfers between devices, body(): w_cols = lax.all_to_all(w_out, 'chan', 1, 0, tiled=True)  6.9 us
    all_to_all x1, starting transfers between devices, body(): proj_t = lax.all_to_all(proj_t, 'ctx', 1, 1, tiled=True)  6.35 us
    all_to_all x1, waiting for transfers between devices, body(): proj_t = lax.all_to_all(proj_t, 'ctx', 1, 1, tiled=True)  6.12 us
  transfers between devices with their start and end apart: 5, of which 4 were waited for; matrix products, arithmetic and copies ran while one was open for 6% of the time, Pallas kernels for 0%

profile of v1, /device:TPU:1, one launch (start us, length us, event | category | flops | bytes accessed | tf_op | source)
XLA Modules:
  0.0 268.2 jit_solution(13815494976643735436)
XLA Ops:
  6.5 0.7 all-gather.2.cloned.1.call-update
  7.3 1.9 copy.19
  9.1 7.5 %all-to-all-start.1 = ((bf16[8,16,512]{2,1,0:T(8,128)(2,1)}), bf16[8,16,512]{2,1,0:T(8,128)(2,1)S(1)}, u32[]{:S(2)}, u32[]{:S(2)}) async-start(bf16[8,16,512]{2,1,0:T(8,128)(2,1)} %bitcast.8), calls=%async_computation.1 | async-start | bytes 262144 | tf_op jit(solution)/shard_map/filter_to_owner/all_to_all | solution.py:35
  16.6 0.5 fusion.47
  17.2 0.6 fusion.50
  17.8 3.5 %negate_convert_fusion = (bf16[32,32,1024]{2,1,0:T(8,128)(2,1)}, bf16[32,32,1024]{2,1,0:T(8,128)(2,1)}) fusion(f32[32,1024]{1,0:T(8,128)S(1)} %get-tuple-element.22, f32[32,1024]{1,0:T(8,128)S(1)} %get-tuple-element.21, f32[32,1024]{1,0:T(8,128)S(1)} %get-tuple-element.23, f32[32,1024]{1,0:T(8,128)S(1)} %get-tuple-element.20), kind=kLoop, calls=%fused_computation.5 | loop fusion | flops 9437184 | bytes 4718592 | tf_op jit(solution)/shard_map/convert.44
  21.3 2.9 %copy.14 = bf16[4096,3,128]{0,2,1:T(8,128)(2,1)} copy(bf16[4096,3,128]{2,0,1:T(8,128)(2,1)S(1)} %copy-done) | data formatting | bytes 6291456 | tf_op args[1]
  24.2 0.1 dynamic_slice.7
  24.3 0.1 fusion.70
  24.3 0.0 all-to-all-done.1
  24.4 0.1 slice.145
  24.5 61.2 %all-gather.2.cloned.1.call-done = bf16[4096,512]{0,1:T(8,128)(2,1)} async-done(((bf16[128,512]{0,1:T(8,128)(2,1)}), bf16[4096,512]{0,1:T(8,128)(2,1)}) %all-gather.2.cloned.1.call-update) | async-done | bytes 4194320 | tf_op jit(solution)/shard_map/input_projection/all_gather | solution.py:37
  85.6 5.1 %convolution_convert_fusion.1 = bf16[384,512]{1,0:T(8,128)(2,1)S(1)} fusion(bf16[4096,384]{0,1:T(8,128)(2,1)} %bitcast.120, bf16[4096,512]{0,1:T(8,128)(2,1)} %all-gather.2.cloned.1.call-done), kind=kOutput, calls=%fused_computation.11 | convolution fusion | flops 1610809344 | bytes 7733248 | tf_op jit(solution)/shard_map/input_projection/dot_general | solution.py:39
  90.7 0.8 copy.15
  91.5 6.4 %all-to-all-start = ((bf16[3,8,16,512]{3,2,0,1:T(8,128)(2,1)}), bf16[3,8,16,512]{3,2,0,1:T(8,128)(2,1)S(1)}, u32[]{:S(2)}, u32[]{:S(2)}) async-start(bf16[3,8,16,512]{3,2,0,1:T(8,128)(2,1)} %copy.15), calls=%async_computation | async-start | bytes 786432 | tf_op jit(solution)/shard_map/projection_to_owner/all_to_all | solution.py:44
  97.9 3.2 %fusion.3 = bf16[8,16,2048]{2,1,0:T(8,128)(2,1)S(1)} fusion(bf16[1024,1024]{1,0:T(8,128)(2,1)S(1)} %bitcast.121, bf16[1024,1024]{1,0:T(8,128)(2,1)} %bitcast.124, bf16[7,16,511]{2,1,0:T(8,128)(2,1)S(1)} %slice.145, bf16[8,16,512]{2,1,0:T(8,128)(2,1)} %copy-done.4, bf16[1024]{0:T(1024)(128)(2,1)S(1)} %pad.29.clone), kind=kOutput, calls=%fused_computation.7 | convolution fusion | flops 546570240 | bytes 4966176 | tf_op jit(solution)/shard_map/spectra/kdm,fm->kdf/dot_general | solution.py:73
  101.1 0.1 slice_convert_fusion.3
  101.2 6.1 %all-to-all-done = bf16[3,8,16,512]{3,2,0,1:T(8,128)(2,1)S(1)} async-done(((bf16[3,8,16,512]{3,2,0,1:T(8,128)(2,1)}), bf16[3,8,16,512]{3,2,0,1:T(8,128)(2,1)S(1)}, u32[]{:S(2)}, u32[]{:S(2)}) %all-to-all-start) | async-done | bytes 393248 | tf_op jit(solution)/shard_map/projection_to_owner/all_to_all | solution.py:44
  107.3 0.1 slice.141
  107.4 0.2 fusion.15
  107.7 0.4 add_convert_fusion
  108.0 2.0 convolution_convert_fusion
  110.1 0.1 slice_convert_fusion.2
  110.2 0.2 fusion.65
  110.4 0.2 fusion.66
  110.5 0.1 fusion.63
  110.7 0.1 fusion.64
  110.8 0.1 fusion.61
  110.9 0.1 fusion.62
  111.1 0.1 fusion.59
  111.2 0.1 fusion.60
  111.2 0.1 fusion.57
  111.3 0.1 fusion.58
  111.4 0.1 fusion.56
  111.5 0.1 fusion.55
  111.5 0.0 copy-start.3
  111.7 1.0 copy-done.2
  112.7 1.1 fusion.11
  113.8 3.4 %all-to-all-start.2 = ((bf16[8,16,512]{2,1,0:T(8,128)(2,1)}), bf16[8,16,512]{2,1,0:T(8,128)(2,1)S(1)}, u32[]{:S(2)}, u32[]{:S(2)}) async-start(bf16[8,16,512]{2,1,0:T(8,128)(2,1)} %fusion.11), calls=%async_computation.2 | async-start | bytes 262144 | tf_op jit(solution)/shard_map/gated_back_to_rows/all_to_all | solution.py:99
  117.2 0.7 copy.21
  117.8 1.3 copy.22
  119.2 4.7 %all-to-all-done.2 = bf16[8,16,512]{2,1,0:T(8,128)(2,1)S(1)} async-done(((bf16[8,16,512]{2,1,0:T(8,128)(2,1)}), bf16[8,16,512]{2,1,0:T(8,128)(2,1)S(1)}, u32[]{:S(2)}, u32[]{:S(2)}) %all-to-all-start.2) | async-done | bytes 131104 | tf_op jit(solution)/shard_map/gated_back_to_rows/all_to_all | solution.py:99
  123.9 6.9 %all-to-all-start.4 = ((bf16[128,32,128]{2,0,1:T(8,128)(2,1)}), bf16[128,32,128]{2,0,1:T(8,128)(2,1)S(1)}, u32[]{:S(2)}, u32[]{:S(2)}) async-start(bf16[128,32,128]{2,0,1:T(8,128)(2,1)} %copy.22), calls=%async_computation.4 | async-start | bytes 2097152 | tf_op jit(solution)/shard_map/out_weight_columns/all_to_all | solution.py:32
  130.8 0.1 copy.20
  130.9 28.0 %all-to-all-done.4 = bf16[128,32,128]{2,0,1:T(8,128)(2,1)S(1)} async-done(((bf16[128,32,128]{2,0,1:T(8,128)(2,1)}), bf16[128,32,128]{2,0,1:T(8,128)(2,1)S(1)}, u32[]{:S(2)}, u32[]{:S(2)}) %all-to-all-start.4) | async-done | bytes 1048608 | tf_op jit(solution)/shard_map/out_weight_columns/all_to_all | solution.py:32
  158.9 0.9 stack.48
  159.9 99.6 %all_to_all.36 = bf16[32,128,512]{1,2,0:T(8,128)(2,1)S(1)} all-to-all(bf16[32,128,512]{1,2,0:T(8,128)(2,1)S(1)} %stack.48), channel_id=1, replica_groups=mesh['ctx'=8,'chan'=32] {'chan'}, dimensions={0} | all-to-all | bytes 8388608 | tf_op jit(solution)/shard_map/output_projection/all_to_all | solution.py:103
  259.5 1.9 fusion.10
  (25 shorter events, 0.1 us)
Async XLA Ops:
  6.5 14.7 %copy-start = (bf16[4096,3,128]{2,0,1:T(8,128)(2,1)S(1)}, bf16[4096,3,128]{2,0,1:T(8,128)(2,1)}, u32[]{:S(2)}) copy-start(bf16[4096,3,128]{2,0,1:T(8,128)(2,1)} %param.7) | copy-start | bytes 9437188
  6.5 79.1 %all-gather.2.cloned.1.call-start = ((), (), s32[]{:S(2)}) async-start(), calls=%async_computation.5 | async-start | bytes 4325376 | tf_op jit(solution)/shard_map/input_projection/all_gather | solution.py:37
  9.1 15.2 %all-to-all-start.1 = ((bf16[8,16,512]{2,1,0:T(8,128)(2,1)}), bf16[8,16,512]{2,1,0:T(8,128)(2,1)S(1)}, u32[]{:S(2)}, u32[]{:S(2)}) async-start(bf16[8,16,512]{2,1,0:T(8,128)(2,1)} %bitcast.8), calls=%async_computation.1 | async-start | bytes 262144 | tf_op jit(solution)/shard_map/filter_to_owner/all_to_all | solution.py:35
  21.3 2.9 %copy-start.6 = (f32[128]{0:T(128)S(1)}, f32[128]{0:T(128)}, u32[]{:S(2)}) copy-start(f32[128]{0:T(128)} %param.9) | copy-start | bytes 1540
  21.3 3.0 %copy-start.5 = (bf16[3,3,128]{2,1,0:T(4,128)(2,1)S(1)}, bf16[3,3,128]{2,1,0:T(4,128)(2,1)}, u32[]{:S(2)}) copy-start(bf16[3,3,128]{2,1,0:T(4,128)(2,1)} %param.8) | copy-start | bytes 6916
  24.4 66.4 %copy-start.4 = (bf16[8,16,512]{2,1,0:T(8,128)(2,1)}, bf16[8,16,512]{2,1,0:T(8,128)(2,1)S(1)}, u32[]{:S(2)}) copy-start(bf16[8,16,512]{2,1,0:T(8,128)(2,1)S(1)} %all-to-all-done.1) | copy-start | bytes 393220
  85.6 12.2 %copy-start.1 = (bf16[32,32,1024]{2,1,0:T(8,128)(2,1)S(1)}, bf16[32,32,1024]{2,1,0:T(8,128)(2,1)}, u32[]{:S(2)}) copy-start(bf16[32,32,1024]{2,1,0:T(8,128)(2,1)} %get-tuple-element.15) | copy-start | bytes 6291460
  91.5 15.8 %all-to-all-start = ((bf16[3,8,16,512]{3,2,0,1:T(8,128)(2,1)}), bf16[3,8,16,512]{3,2,0,1:T(8,128)(2,1)S(1)}, u32[]{:S(2)}, u32[]{:S(2)}) async-start(bf16[3,8,16,512]{3,2,0,1:T(8,128)(2,1)} %copy.15), calls=%async_computation | async-start | bytes 786432 | tf_op jit(solution)/shard_map/projection_to_owner/all_to_all | solution.py:44
  111.1 1.6 copy-start.2
  111.5 5.6 %copy-start.3 = (bf16[128,4096]{1,0:T(8,128)(2,1)S(1)}, bf16[128,4096]{1,0:T(8,128)(2,1)}, u32[]{:S(2)}) copy-start(bf16[128,4096]{1,0:T(8,128)(2,1)} %param.11) | copy-start | bytes 3145732
  113.8 10.1 %all-to-all-start.2 = ((bf16[8,16,512]{2,1,0:T(8,128)(2,1)}), bf16[8,16,512]{2,1,0:T(8,128)(2,1)S(1)}, u32[]{:S(2)}, u32[]{:S(2)}) async-start(bf16[8,16,512]{2,1,0:T(8,128)(2,1)} %fusion.11), calls=%async_computation.2 | async-start | bytes 262144 | tf_op jit(solution)/shard_map/gated_back_to_rows/all_to_all | solution.py:99
  123.9 35.0 %all-to-all-start.4 = ((bf16[128,32,128]{2,0,1:T(8,128)(2,1)}), bf16[128,32,128]{2,0,1:T(8,128)(2,1)S(1)}, u32[]{:S(2)}, u32[]{:S(2)}) async-start(bf16[128,32,128]{2,0,1:T(8,128)(2,1)} %copy.22), calls=%async_computation.4 | async-start | bytes 2097152 | tf_op jit(solution)/shard_map/out_weight_columns/all_to_all | solution.py:32
Sparse Core Ops, SparseCore 0:
  9.1 76.4 all-gather.1
